TPU v7x, 32 devices: a whole 2x2x4 slice. The times are simulated.
32 devices in a mesh: ctx: 8 (over y, x, core), grp: 4 (over z).
Axes of the slice: x: 2, y: 2, z: 4, core: 2. Of those that a mesh axis runs over, the one named last changes fastest.
Arguments:
- query_in: bfloat16 [8192, 4096], P('ctx', 'grp'), may hold values from -6 to 6
- key_in: bfloat16 [8192, 4096], P('ctx', 'grp'), may hold values from -6 to 6
- value_in: bfloat16 [8192, 4096], P('ctx', 'grp'), may hold values from -6 to 6
- residues: float32 [256, 16], P('grp'), may hold values from -1.5 to 1.5
- decay_time: float32 [256, 16], P('grp'), may hold values from 20 to 32768
- skip_gain: float32 [4096], P('grp'), may hold values from 0.5 to 1.5
- out_proj: bfloat16 [4096, 4096], P('ctx', 'grp'), may hold values from -0.09375 to 0.09375
- doc_lengths: int32 [4], replicated, may hold values from 1 to 4096, 8192 in all
- grad_out: bfloat16 [8192, 4096], P('ctx', 'grp'), may hold values from -6 to 6
Outputs:
- mixed_out: bfloat16 [8192, 4096], P('ctx', 'grp')
- grad_query: bfloat16 [8192, 4096], P('ctx', 'grp')
- grad_key: bfloat16 [8192, 4096], P('ctx', 'grp')
- grad_value: bfloat16 [8192, 4096], P('ctx', 'grp')
- grad_proj: float32 [4096, 4096], P('ctx', 'grp')
Inputs may be any that keep to these rules, and one draw needn't show every extreme that they name: `doc_lengths`: document lengths in window order, summing to 8192; the longest is exactly 4096.
All inputs are finite; a program needn't handle non-finite values.
Results may differ from a plain program's by a relative error of at most 0.013.
Values may be sent and summed in bfloat16 or wider, within the bound.
A program may use at most 192 MiB of HBM per device.

v0:
```python
import jax
import jax.numpy as jnp
from jax import lax
from jax.sharding import PartitionSpec as P


def prefix(value, axis, combine, identity, reverse):
    size, position = (lax.axis_size(axis), lax.axis_index(axis))
    everything = jax.tree.map(
        lambda part, kind: lax.all_gather(part.astype(kind), axis),
        value,
        jax.tree.map(lambda a: jnp.bfloat16 if a.dtype == jnp.float32 else a.dtype, value),
    )
    start = jax.tree.map(
        lambda part, zero: jnp.broadcast_to(jnp.asarray(zero, part.dtype), part.shape),
        value,
        identity,
    )

    def step(k, before):
        at = size - 1 - k if reverse else k
        reached = at > position if reverse else at < position
        new = combine(
            before, jax.tree.map(lambda part, own: part[at].astype(own.dtype), everything, value)
        )
        return jax.tree.map(lambda a, b: jnp.where(reached, a, b), new, before)

    return lax.fori_loop(0, size, step, start)


def chain(former, latter):
    return (former[0] * latter[0], latter[0][:, None, :] * former[1] + latter[1])


def doc_index(starts, where_now):
    return jnp.sum((starts[None, :] <= where_now[:, None]).astype(jnp.int32), axis=1) - 1


def local(
    query_in, key_in, value_in, residues, decay_time, skip_gain, out_proj, doc_lengths, grad_out
):
    tok_rows, channels = query_in.shape
    filters, poles = residues.shape
    members = channels // filters
    block_len = min(128, tok_rows)
    block_count = tok_rows // block_len
    starts = jnp.cumsum(doc_lengths) - doc_lengths
    where_now = lax.axis_index("ctx") * tok_rows + jnp.arange(tok_rows, dtype=jnp.int32)
    doc_ids = doc_index(starts, where_now).reshape(block_count, block_len)
    prior_ids = doc_index(starts, where_now - 1).reshape(block_count, block_len)[:, 0]
    decay_rate = 1.0 / decay_time
    residue_scaled = residues * jnp.sqrt(-jnp.expm1(-2.0 * decay_rate))
    lag_steps = jnp.arange(block_len, dtype=jnp.float32)
    powers = jnp.exp(-lag_steps[None, None, :] * decay_rate[:, :, None])
    lagged = jnp.sum(residue_scaled[:, :, None] * powers, axis=1)
    positions = jnp.arange(block_len, dtype=jnp.int32)
    lag_index = jnp.clip(positions[:, None] - positions[None, :], 0, block_len - 1)
    toeplitz = jnp.take(lagged, lag_index, axis=1)
    causal = positions[:, None] >= positions[None, :]
    same_docs = (doc_ids[:, :, None] == doc_ids[:, None, :]) & causal[None]
    masked = toeplitz[None] * same_docs[:, None].astype(jnp.float32)
    step_enter = jnp.exp(-(lag_steps + 1.0)[None, None, :] * decay_rate[:, :, None])
    alive_enter = (doc_ids == prior_ids[:, None]).astype(jnp.float32)
    enter_gain = residue_scaled[None, :, :, None] * step_enter[None] * alive_enter[:, None, None, :]
    step_leave = jnp.exp(-(block_len - 1.0 - lag_steps)[None, None, :] * decay_rate[:, :, None])
    alive_leave = (doc_ids == doc_ids[:, -1:]).astype(jnp.float32)
    leave_gain = step_leave[None] * alive_leave[:, None, None, :]
    across_gain = (
        jnp.exp(-block_len * decay_rate)[None]
        * (prior_ids == doc_ids[:, -1]).astype(jnp.float32)[:, None, None]
    )
    unit_decay = jnp.ones((filters, poles), jnp.float32)
    empty_state = jnp.zeros((filters, members, poles), jnp.float32)
    highest = lax.Precision.HIGHEST
    query_f = query_in.astype(jnp.float32)
    key_f = key_in.astype(jnp.float32)
    value_f = value_in.astype(jnp.float32)
    product_f = (key_f * value_f).astype(jnp.bfloat16).astype(jnp.float32)
    gathered = lax.all_gather(out_proj, "ctx", axis=0, tiled=True)
    shaped = product_f.reshape(block_count, block_len, filters, members)
    within = jnp.einsum("bgts,bsgc->btgc", masked, shaped, precision=highest)
    block_state = jnp.einsum("bgns,bsgc->bgcn", leave_gain, shaped, precision=highest)
    summary = (unit_decay, empty_state)
    for number in range(block_count):
        summary = chain(summary, (across_gain[number], block_state[number]))
    incoming = prefix(summary, "ctx", chain, (unit_decay, empty_state), False)[1]
    entering = []
    for number in range(block_count):
        entering.append(incoming)
        incoming = across_gain[number][:, None, :] * incoming + block_state[number]
    beyond = jnp.einsum("bgnt,bgcn->btgc", enter_gain, jnp.stack(entering), precision=highest)
    convolved = (within + beyond).reshape(tok_rows, channels)
    grad_full = lax.all_gather(grad_out, "grp", axis=1, tiled=True)
    grad_gated = jnp.dot(grad_full, gathered, preferred_element_type=jnp.float32)
    grad_filtered = grad_gated * query_f
    shaped = grad_filtered.reshape(block_count, block_len, filters, members)
    within = jnp.einsum("bgts,btgc->bsgc", masked, shaped, precision=highest)
    block_adjoint = jnp.einsum("bgnt,btgc->bgcn", enter_gain, shaped, precision=highest)
    summary = (unit_decay, empty_state)
    for number in reversed(range(block_count)):
        summary = chain(summary, (across_gain[number], block_adjoint[number]))
    incoming = prefix(summary, "ctx", chain, (unit_decay, empty_state), True)[1]
    leaving = [None] * block_count
    for number in reversed(range(block_count)):
        leaving[number] = incoming
        incoming = block_adjoint[number] + across_gain[number][:, None, :] * incoming
    beyond = jnp.einsum("bgns,bgcn->bsgc", leave_gain, jnp.stack(leaving), precision=highest)
    grad_product = (within + beyond).reshape(tok_rows, channels) + skip_gain * grad_filtered
    grad_full, grad_gated, grad_product = (grad_full, grad_gated, grad_product)
    filtered = convolved + skip_gain * product_f
    gated = (query_f * filtered).astype(jnp.bfloat16)
    partial_value = lax.dot_general(
        gated, gathered, (((1,), (1,)), ((), ())), preferred_element_type=jnp.float32
    )
    rounded = lax.optimization_barrier(partial_value.astype(jnp.bfloat16)).astype(jnp.float32)
    mixed_out = lax.psum_scatter(
        rounded.astype(jnp.bfloat16), "grp", scatter_dimension=1, tiled=True
    )
    grad_query = (grad_gated * filtered).astype(jnp.bfloat16)
    grad_key = (grad_product * value_f).astype(jnp.bfloat16)
    grad_value = (grad_product * key_f).astype(jnp.bfloat16)
    term_whole = lax.dot_general(
        grad_full, gated, (((0,), (0,)), ((), ())), preferred_element_type=jnp.float32
    )
    grad_proj = lax.psum_scatter(
        term_whole.astype(jnp.bfloat16), "ctx", scatter_dimension=0, tiled=True
    ).astype(jnp.float32)
    return (mixed_out, grad_query, grad_key, grad_value, grad_proj)


def solution(mesh):
    return jax.shard_map(
        local,
        mesh=mesh,
        in_specs=(
            P("ctx", "grp"),
            P("ctx", "grp"),
            P("ctx", "grp"),
            P("grp", None),
            P("grp", None),
            P("grp"),
            P("ctx", "grp"),
            P(),
            P("ctx", "grp"),
        ),
        out_specs=(
            P("ctx", "grp"),
            P("ctx", "grp"),
            P("ctx", "grp"),
            P("ctx", "grp"),
            P("ctx", "grp"),
        ),
        check_vma=False,
    )
```

profile of v0, /device:TPU:0, one launch (start us, length us, event | category | flops | bytes accessed | tf_op | source)
XLA Modules:
  0.0 472.9 jit_solution(16849011690872754440)
XLA Ops:
  8.7 0.8 reduce-window.9
  11.7 3.9 fusion.20
  15.6 3.9 copy.180
  19.5 2.5 copy.219
  25.1 1.8 multiply_reduce_fusion
  26.9 3.4 fusion.16
  30.3 2.1 copy-done.3
  32.4 1.1 fusion.39
  33.5 1.8 copy.195
  35.3 10.7 %all_gather.22 = bf16[8,64,16]{1,2,0:T(8,128)(2,1)S(1)} all-gather(bf16[1,64,16]{1,2,0:T(8,128)(2,1)} %get-tuple-element.365), channel_id=1, replica_groups=mesh['ctx'=8,'grp'=4] {'ctx'}, dimensions={0}, use_global_device_ids=true | all-gather | bytes 18432 | tf_op jit(solution)/shard_map/all_gather | solution.py:10
  46.0 9.9 %all_gather.23 = bf16[8,64,16,16]{1,3,2,0:T(8,128)(2,1)S(1)} all-gather(bf16[1,64,16,16]{1,3,2,0:T(8,128)(2,1)} %copy.195), channel_id=1, replica_groups=mesh['ctx'=8,'grp'=4] {'ctx'}, dimensions={0}, use_global_device_ids=true | all-gather | bytes 294912 | tf_op jit(solution)/shard_map/all_gather | solution.py:10
  56.9 0.8 copy.197
  57.7 0.8 copy.183
  58.6 54.4 %gather_fusion = f32[16384,64]{1,0:T(8,128)} fusion(f32[64,128]{0,1:T(8,128)S(1)} %copy.183, s32[16384]{0:T(1024)S(1)} %fusion.41), kind=kCustom, calls=%fused_computation | custom fusion | bytes 8454144 | tf_op jit(solution)/shard_map/jit(_take)/gather | solution.py:58
  113.0 10.0 %select_bitcast_fusion = f32[64,128,128]{0,2,1:T(8,128)} fusion(f32[128,128,64]{2,1,0:T(8,128)} %bitcast.199, pred[128,128]{1,0:T(8,128)(4,1)S(1)} %fusion.44), kind=kLoop, calls=%fused_computation.15 | loop fusion | flops 1048576 | bytes 8404992 | tf_op jit(solution)/shard_map/jit(_take)/select_n | solution.py:58
  123.0 7.3 %copy.184 = f32[64,128,128]{2,1,0:T(8,128)} copy(f32[64,128,128]{0,2,1:T(8,128)} %select_bitcast_fusion) | data formatting | bytes 8388608 | tf_op jit(solution)/shard_map/jit(_take)/select_n | solution.py:58
  130.6 1.5 bitcast_dynamic-update-slice_fusion.14
  132.1 1.3 bitcast_dynamic-update-slice_fusion.13
  134.1 5.2 %fusion.12 = f32[8,64,16,128]{3,2,1,0:T(8,128)S(1)} fusion(f32[8,64,16,16]{3,2,1,0:T(8,128)S(1)} %bitcast_dynamic-update-slice_fusion.8, f32[8,128]{1,0:T(8,128)S(1)} %get-tuple-element.379, f32[64,16,128]{2,1,0:T(8,128)S(1)} %get-tuple-element.369), kind=kOutput, calls=%fused_computation.20 | convolution fusion | flops 202375168 | bytes 5246976 | tf_op jit(solution)/shard_map/bgnt,bgcn->btgc/dot_general | solution.py:91
  139.3 26.9 %add_bitcast_fusion.1 = f32[8,128,64,16]{1,3,2,0:T(8,128)S(1)} fusion(f32[8,64,16,128]{3,2,1,0:T(8,128)S(1)} %fusion.12, f32[8,128,128]{2,1,0:T(8,128)S(1)} %and_convert_fusion, f32[64,128,128]{2,1,0:T(8,128)S(1)} %copy-done, bf16[8,128,64,16]{1,0,3,2:T(8,128)(2,1)S(1)} %bitcast.198), kind=kOutput, calls=%fused_computation.41 | convolution fusion | flops 1620049920 | bytes 15204352 | tf_op jit(solution)/shard_map/bgts,bsgc->btgc/dot_general | solution.py:81
  166.2 2.4 copy.205
  168.7 3.0 copy.235
  171.6 5.5 %copy.206 = f32[1024,1024]{1,0:T(8,128)} copy(f32[1024,1024]{0,1:T(8,128)} %bitcast.201) | data formatting | bytes 8388608 | tf_op jit(solution)/shard_map/reshape | solution.py:92
  177.2 39.3 %all-gather.3.cloned.1.call-done = bf16[4096,1024]{1,0:T(8,128)(2,1)} async-done(((bf16[512,1024]{1,0:T(8,128)(2,1)}), bf16[4096,1024]{1,0:T(8,128)(2,1)}) %all-gather.3.cloned.1.call-update) | async-done | bytes 8388624 | tf_op jit(solution)/shard_map/all_gather | solution.py:79
  216.5 17.4 %multiply_convert_fusion = (bf16[1024,1024]{1,0:T(8,128)(2,1)}, bf16[1024,1024]{1,0:T(8,128)(2,1)S(1)}, f32[1024,1024]{1,0:T(8,128)}) fusion(f32[1024,1024]{1,0:T(8,128)} %copy.206, bf16[1024,1024]{1,0:T(8,128)(2,1)S(1)} %copy-done.9, f32[1024]{0:T(1024)S(1)} %copy-done.17, bf16[1024,1024]{1,0:T(8,128)(2,1)} %param.13, ...), kind=kOutput, calls=%fused_computation.39 | convolution fusion | flops 8599371776 | bytes 33558528 | tf_op jit(solution)/shard_map/dot_general | solution.py:94
  233.9 1.3 copy-done.20
  235.2 11.4 %convert_bitcast_fusion = bf16[4096,1024]{0,1:T(8,128)(2,1)} fusion(bf16[1024,1024]{1,0:T(8,128)(2,1)S(1)} %get-tuple-element.359, bf16[1024,4096]{1,0:T(8,128)(2,1)S(1)} %copy-done.18), kind=kOutput, calls=%fused_computation.16 | convolution fusion | flops 8594128896 | bytes 18874368 | tf_op jit(solution)/shard_map/dot_general | solution.py:122
  246.7 1.5 copy-done.21
  248.2 14.5 %convolution_convert_fusion = bf16[1024,4096]{1,0:T(8,128)(2,1)} fusion(bf16[1024,1024]{1,0:T(8,128)(2,1)S(1)} %copy-done.21, bf16[4096,1024]{1,0:T(8,128)(2,1)} %all-gather.3.cloned.1.call-done), kind=kOutput, calls=%fused_computation.17 | convolution fusion | flops 8594128896 | bytes 18874368 | tf_op jit(solution)/shard_map/dot_general | solution.py:112
  263.4 9.0 %all_gather.26 = bf16[8,64,16]{1,2,0:T(8,128)(2,1)S(1)} all-gather(bf16[1,64,16]{1,2,0:T(8,128)(2,1)S(1)} %get-tuple-element.363), channel_id=1, replica_groups=mesh['ctx'=8,'grp'=4] {'ctx'}, dimensions={0}, use_global_device_ids=true | all-gather | bytes 18432 | tf_op jit(solution)/shard_map/all_gather | solution.py:10
  272.4 5.3 %copy.207 = f32[1024,1024]{0,1:T(8,128)} copy(f32[1024,1024]{1,0:T(8,128)} %get-tuple-element.360) | data formatting | bytes 8388608 | tf_op jit(solution)/shard_map/mul | solution.py:95
  277.8 3.4 copy.221
  281.2 7.0 %fusion.10 = f32[8,64,16,16]{3,2,1,0:T(8,128)S(1)} fusion(f32[8,128,64,16]{1,0,3,2:T(8,128)S(1)} %bitcast.195, f32[8,128]{1,0:T(8,128)S(1)} %get-tuple-element.379, f32[64,16,128]{2,1,0:T(8,128)S(1)} %get-tuple-element.369), kind=kOutput, calls=%fused_computation.18 | convolution fusion | flops 202375168 | bytes 5246976 | tf_op jit(solution)/shard_map/bgnt,btgc->bgcn/dot_general | solution.py:98
  288.2 2.0 copy-done.2
  290.9 10.2 %all_gather.27 = bf16[8,64,16,16]{1,3,2,0:T(8,128)(2,1)S(1)} all-gather(bf16[1,64,16,16]{1,3,2,0:T(8,128)(2,1)S(1)} %copy.213), channel_id=1, replica_groups=mesh['ctx'=8,'grp'=4] {'ctx'}, dimensions={0}, use_global_device_ids=true | all-gather | bytes 294912 | tf_op jit(solution)/shard_map/all_gather | solution.py:10
  301.1 0.8 while.31
  302.2 2.7 bitcast_dynamic-update-slice_fusion.7
  304.9 1.3 bitcast_dynamic-update-slice_fusion.6
  306.3 1.8 bitcast_dynamic-update-slice_fusion.4
  308.1 1.1 bitcast_dynamic-update-slice_fusion.2
  309.4 29.0 %fusion.2 = f32[8,64,16,128]{3,2,1,0:T(8,128)S(1)} fusion(f32[8,128,128]{2,1,0:T(8,128)S(1)} %copy-done.11, f32[64,128,128]{2,1,0:T(8,128)S(1)} %copy-done.1, f32[8,128,64,16]{1,0,3,2:T(8,128)S(1)} %bitcast.196), kind=kOutput, calls=%fused_computation.7 | convolution fusion | flops 1619001344 | bytes 13107200 | tf_op jit(solution)/shard_map/bgts,btgc->bsgc/dot_general | solution.py:97
  338.4 5.0 %add_bitcast_fusion = f32[8,128,64,16]{1,3,2,0:T(8,128)S(1)} fusion(f32[8,64,16,128]{3,2,1,0:T(8,128)S(1)} %fusion.2, f32[8,64,16,16]{3,2,1,0:T(8,128)S(1)} %bitcast_dynamic-update-slice_fusion, f32[8,128]{1,0:T(8,128)S(1)} %get-tuple-element.380, f32[64,16,128]{2,1,0:T(8,128)S(1)} %copy-done.13), kind=kOutput, calls=%fused_computation.38 | convolution fusion | flops 203423744 | bytes 9441280 | tf_op jit(solution)/shard_map/bgns,bgcn->bsgc/dot_general | solution.py:107
  343.4 2.4 copy.216
  345.8 3.0 copy.234
  348.8 5.5 %copy.217 = f32[1024,1024]{1,0:T(8,128)} copy(f32[1024,1024]{0,1:T(8,128)} %bitcast.203) | data formatting | bytes 8388608 | tf_op jit(solution)/shard_map/reshape | solution.py:108
  354.3 7.8 %fusion.19 = (bf16[1024,1024]{1,0:T(8,128)(2,1)}, bf16[1024,1024]{1,0:T(8,128)(2,1)}) fusion(bf16[1024,1024]{1,0:T(8,128)(2,1)} %param.14, f32[1024,1024]{1,0:T(8,128)} %copy.217, f32[1024,1024]{1,0:T(8,128)} %get-tuple-element.360, f32[1024]{0:T(1024)S(1)} %copy-done.17, bf16[1024,1024]{1,0:T(8,128)(2,1)S(1)} %copy-done.8), kind=kLoop, calls=%fused_computation.32 | loop fusion | flops 8388608 | bytes 16781312 | tf_op jit(solution)/shard_map/convert_element_type | solution.py:121
  362.1 2.6 copy.218
  364.7 101.5 %reduce-scatter.3.cloned.1.call-done = bf16[1024,1024]{1,0:T(8,128)(2,1)} async-done(((bf16[1024,4096]{1,0:T(8,128)(2,1)}), bf16[1024,1024]{1,0:T(8,128)(2,1)}) %reduce-scatter.3.cloned.1.call-update) | async-done | bytes 2097168 | tf_op jit(solution)/shard_map/reduce_scatter | solution.py:116
  (130 shorter events, 11.7 us)
Async XLA Ops:
  7.2 4.5 copy-start.7
  7.2 170.0 %all-gather.5.cloned.1.call-start = ((), (), s32[]{:S(2)}) async-start(), calls=%async_computation.4 | async-start | bytes 10485760 | tf_op jit(solution)/shard_map/all_gather | solution.py:93
  7.9 208.5 %all-gather.3.cloned.1.call-start = ((), (), s32[]{:S(2)}) async-start(), calls=%async_computation.2 | async-start | bytes 9437184 | tf_op jit(solution)/shard_map/all_gather | solution.py:79
  8.7 353.4 %reduce-scatter.5.cloned.1.call-start = ((), (), s32[]{:S(2)}) async-start(), calls=%async_computation.5 | async-start | bytes 9437184 | tf_op jit(solution)/shard_map/reduce_scatter | solution.py:125
  15.6 6.5 %copy-start.19 = (s32[4]{0:T(128)S(1)}, s32[4]{0:T(128)}, u32[]{:S(2)}) copy-start(s32[4]{0:T(128)} %param.20) | copy-start | bytes 52
  25.0 8.5 %copy-start.14 = (f32[64,16]{1,0:T(8,128)}, f32[64,16]{1,0:T(8,128)S(1)}, u32[]{:S(2)}) copy-start(f32[64,16]{1,0:T(8,128)S(1)} %copy.186) | copy-start | bytes 12292
  26.9 6.6 %copy-start.12 = (f32[64,16,128]{2,1,0:T(8,128)}, f32[64,16,128]{2,1,0:T(8,128)S(1)}, u32[]{:S(2)}) copy-start(f32[64,16,128]{2,1,0:T(8,128)S(1)} %get-tuple-element.375) | copy-start | bytes 1572868
  30.3 2.1 copy-start.3
  130.3 3.1 copy-start.4
  130.6 8.7 %copy-start.10 = (f32[8,128,128]{2,1,0:T(8,128)}, f32[8,128,128]{2,1,0:T(8,128)S(1)}, u32[]{:S(2)}) copy-start(f32[8,128,128]{2,1,0:T(8,128)S(1)} %and_convert_fusion) | copy-start | bytes 1572868
  134.1 5.2 %copy-start = (f32[64,128,128]{2,1,0:T(8,128)S(1)}, f32[64,128,128]{2,1,0:T(8,128)}, u32[]{:S(2)}) copy-start(f32[64,128,128]{2,1,0:T(8,128)} %copy.184) | copy-start | bytes 12582916
  171.6 44.8 %copy-start.9 = (bf16[1024,1024]{1,0:T(8,128)(2,1)S(1)}, bf16[1024,1024]{1,0:T(8,128)(2,1)}, u32[]{:S(2)}) copy-start(bf16[1024,1024]{1,0:T(8,128)(2,1)} %fusion.20) | copy-start | bytes 6291460
  171.6 44.8 %copy-start.17 = (f32[1024]{0:T(1024)S(1)}, f32[1024]{0:T(1024)}, u32[]{:S(2)}) copy-start(f32[1024]{0:T(1024)} %param.18) | copy-start | bytes 12292
  216.5 18.8 %copy-start.18 = (bf16[1024,4096]{1,0:T(8,128)(2,1)S(1)}, bf16[1024,4096]{1,0:T(8,128)(2,1)}, u32[]{:S(2)}) copy-start(bf16[1024,4096]{1,0:T(8,128)(2,1)} %all-gather.5.cloned.1.call-done) | copy-start | bytes 25165828
  233.9 1.3 copy-start.20
  246.6 1.6 copy-start.21
  246.6 219.5 %reduce-scatter.3.cloned.1.call-start = ((), (), s32[]{:S(2)}) async-start(), calls=%async_computation.3 | async-start | bytes 10485760 | tf_op jit(solution)/shard_map/reduce_scatter | solution.py:116
  262.7 0.7 copy-start.16
  281.2 7.0 %copy-start.5 = (f32[128,8,8,128]{3,2,1,0:T(8,128)}, f32[128,8,8,128]{3,2,1,0:T(8,128)S(1)}, u32[]{:S(2)}) copy-start(f32[128,8,8,128]{3,2,1,0:T(8,128)S(1)} %copy.221) | copy-start | bytes 12582916
  288.2 2.0 copy-start.2
  290.2 11.9 %copy-start.15 = (f32[64,16]{1,0:T(8,128)S(1)}, f32[64,16]{1,0:T(8,128)}, u32[]{:S(2)}) copy-start(f32[64,16]{1,0:T(8,128)} %copy-done.14) | copy-start | bytes 12292
  304.9 4.5 copy-start.1
  304.9 4.5 copy-start.6
  304.9 4.5 copy-start.11
  309.4 29.0 %copy-start.13 = (f32[64,16,128]{2,1,0:T(8,128)S(1)}, f32[64,16,128]{2,1,0:T(8,128)}, u32[]{:S(2)}) copy-start(f32[64,16,128]{2,1,0:T(8,128)} %copy-done.12) | copy-start | bytes 1572868
  348.8 5.5 %copy-start.8 = (bf16[1024,1024]{1,0:T(8,128)(2,1)S(1)}, bf16[1024,1024]{1,0:T(8,128)(2,1)}, u32[]{:S(2)}) copy-start(bf16[1024,1024]{1,0:T(8,128)(2,1)} %param.15) | copy-start | bytes 6291460
Sparse Core Ops, SparseCore 0:
  9.6 152.3 all-gather.4
  163.8 52.5 all-gather.2
  246.8 71.9 reduce-scatter.4
  321.7 144.4 reduce-scatter.2
where the time goes:
time: 480 us; the launch traced here: 473 us
  waiting for transfers between devices  142 us (30%)
  matrix products  120 us (25%)
  local copies, waits for them, and re-layouts  116 us (24%)
  other arithmetic  39.7 us (8%)
  blocking collectives  39.7 us (8%)
  between operations  14.4 us (3%)
    reduce_scatter x1, waiting for transfers between devices, local(): lax.psum_scatter(rounded.astype(jnp.bfloat16), 'grp', scatter_dimension=1...  101 us
    gather x1, local copies, waits for them, and re-layouts, local(): toeplitz = jnp.take(lagged, lag_index, axis=1)  54.4 us
    all_gather x4, blocking collectives, prefix(): lax.all_gather(part.astype(kind), axis)  39.7 us
    all_gather x1, waiting for transfers between devices, local(): gathered = lax.all_gather(out_proj, 'ctx', axis=0, tiled=True)  39.3 us
    dot_general x1, matrix products, local(): within = jnp.einsum('bgts,btgc->bsgc', masked, shaped, precision=highest)  29 us
    dot_general x1, matrix products, local(): within = jnp.einsum('bgts,bsgc->btgc', masked, shaped, precision=highest)  26.9 us
    unnamed x53, local copies, waits for them, and re-layouts  22.2 us
    dot_general x1, matrix products, local(): jnp.dot(grad_full, gathered, preferred_element_type=jnp.float32)  17.4 us
  transfers between devices with their start and end apart: 4, of which 2 were waited for; matrix products, arithmetic and copies ran while one was open for 51% of the time, Pallas kernels for 0%

commit v1 on v0

--- a/solution.py
+++ b/solution.py
@@ -76,7 +76,16 @@
     key_f = key_in.astype(jnp.float32)
     value_f = value_in.astype(jnp.float32)
     product_f = (key_f * value_f).astype(jnp.bfloat16).astype(jnp.float32)
-    gathered = lax.all_gather(out_proj, "ctx", axis=0, tiled=True)
+    size_here = lax.axis_size("ctx")
+    pile = [out_proj]
+    for w in range(size_here - 1):
+        wide_out = lax.ppermute(
+            pile[-1], "ctx", perm=[(dev_j, (dev_j + 1) % size_here) for dev_j in range(size_here)]
+        )
+        pile.append(wide_out)
+    x_new = jnp.concatenate(pile[::-1], axis=0)
+    back = lax.axis_index("ctx")
+    gathered = jnp.roll(x_new, shift=(back + 1) * out_proj.shape[0], axis=0)
     shaped = product_f.reshape(block_count, block_len, filters, members)
     within = jnp.einsum("bgts,bsgc->btgc", masked, shaped, precision=highest)
     block_state = jnp.einsum("bgns,bsgc->bgcn", leave_gain, shaped, precision=highest)

time: 480 us -> 615 us (1.28)
  waiting for transfers between devices: 142 us -> 228 us
  local copies, waits for them, and re-layouts: 116 us -> 145 us
  other arithmetic: 39.7 us -> 55.7 us
    unnamed x53 -> x120, local copies, waits for them, and re-layouts: 22.2 us -> 67.7 us
    reduce_scatter x1, waiting for transfers between devices: 0.01 us -> 45 us  [local(): lax.psum_scatter(term_whole.astype(jnp.bfloat16), 'ctx', scatter_dimensio...]
    reduce_scatter x1, waiting for transfers between devices: 101 us -> 145 us  [local(): lax.psum_scatter(rounded.astype(jnp.bfloat16), 'grp', scatter_dimension=1...]
    all_gather x1 -> x0, waiting for transfers between devices: 39.3 us -> none  [local(): gathered = lax.all_gather(out_proj, 'ctx', axis=0, tiled=True)]
    ppermute x0 -> x7, waiting for transfers between devices: none -> 37 us  [local(): lax.ppermute(pile[-1], 'ctx', perm=[(dev_j, (dev_j + 1) % size_here) for...]
    reshape x2 -> x0, local copies, waits for them, and re-layouts: 11 us -> none  [the longest x1 5.53 us: local(): convolved = (within + beyond).reshape(tok_rows, channels)]
    unnamed x12, other arithmetic: 10.2 us -> 17.5 us
    select_n x16, other arithmetic: 0.93 us -> 7.65 us  [step(): return jax.tree.map(lambda a, b: jnp.where(reached, a, b), new, before)]
  transfers between devices with their start and end apart: 4 -> 10, of which waited for: 2 -> 6; matrix products, arithmetic and copies ran while one was open for 51% -> 28% of each run, Pallas kernels for 0% -> 0%
where the time goes in v1:
time: 615 us; the launch traced here: 604 us
  waiting for transfers between devices  228 us (37%)
  local copies, waits for them, and re-layouts  145 us (24%)
  matrix products  118 us (19%)
  other arithmetic  55.7 us (9%)
  blocking collectives  40.6 us (7%)
  between operations  14.6 us (2%)
    reduce_scatter x1, waiting for transfers between devices, local(): lax.psum_scatter(rounded.astype(jnp.bfloat16), 'grp', scatter_dimension=1...  145 us
    unnamed x120, local copies, waits for them, and re-layouts  67.7 us
    gather x1, local copies, waits for them, and re-layouts, local(): toeplitz = jnp.take(lagged, lag_index, axis=1)  54.4 us
    reduce_scatter x1, waiting for transfers between devices, local(): lax.psum_scatter(term_whole.astype(jnp.bfloat16), 'ctx', scatter_dimensio...  45 us
    all_gather x4, blocking collectives, prefix(): lax.all_gather(part.astype(kind), axis)  40.6 us
    ppermute x7, waiting for transfers between devices, local(): lax.ppermute(pile[-1], 'ctx', perm=[(dev_j, (dev_j + 1) % size_here) for...  37 us
    dot_general x1, matrix products, local(): within = jnp.einsum('bgts,btgc->bsgc', masked, shaped, precision=highest)  28.8 us
    dot_general x1, matrix products, local(): within = jnp.einsum('bgts,bsgc->btgc', masked, shaped, precision=highest)  26.4 us
  transfers between devices with their start and end apart: 10, of which 6 were waited for; matrix products, arithmetic and copies ran while one was open for 28% of the time, Pallas kernels for 0%

profile of v1, /device:TPU:0, one launch (start us, length us, event | category | flops | bytes accessed | tf_op | source)
XLA Modules:
  0.0 604.0 jit_solution(7518295023820282792)
XLA Ops:
  8.5 2.9 copy.193
  11.4 4.6 copy.194
  16.3 7.8 %collective-permute-done = bf16[512,1024]{1,0:T(8,128)(2,1)S(1)} collective-permute-done((bf16[512,1024]{1,0:T(8,128)(2,1)}, bf16[512,1024]{1,0:T(8,128)(2,1)S(1)}, u32[]{:S(2)}, u32[]{:S(2)}) %collective-permute-start) | collective-permute-done | bytes 1048608 | tf_op jit(solution)/shard_map/ppermute | solution.py:82
  24.4 4.1 fusion.52
  28.5 10.7 %collective-permute-done.1 = bf16[512,1024]{1,0:T(8,128)(2,1)} collective-permute-done((bf16[512,1024]{1,0:T(8,128)(2,1)S(1)}, bf16[512,1024]{1,0:T(8,128)(2,1)}, u32[]{:S(2)}, u32[]{:S(2)}) %collective-permute-start.1) | collective-permute-done | bytes 1048608 | tf_op jit(solution)/shard_map/ppermute | solution.py:82
  40.7 2.2 copy.233
  46.2 8.5 %collective-permute-done.2 = bf16[512,1024]{1,0:T(8,128)(2,1)} collective-permute-done((bf16[512,1024]{1,0:T(8,128)(2,1)}, bf16[512,1024]{1,0:T(8,128)(2,1)}, u32[]{:S(2)}, u32[]{:S(2)}) %collective-permute-start.2) | collective-permute-done | bytes 1048608 | tf_op jit(solution)/shard_map/ppermute | solution.py:82
  57.3 3.4 fusion.19
  60.7 2.1 copy-done.2
  63.5 9.8 %all_gather.19 = bf16[8,64,16]{1,2,0:T(8,128)(2,1)S(1)} all-gather(bf16[1,64,16]{1,2,0:T(8,128)(2,1)S(1)} %get-tuple-element.366), channel_id=1, replica_groups=mesh['ctx'=8,'grp'=4] {'ctx'}, dimensions={0}, use_global_device_ids=true | all-gather | bytes 18432 | tf_op jit(solution)/shard_map/all_gather | solution.py:10
  73.4 9.8 %all_gather.20 = bf16[8,64,16,16]{1,3,2,0:T(8,128)(2,1)S(1)} all-gather(bf16[1,64,16,16]{1,3,2,0:T(8,128)(2,1)S(1)} %copy.209), channel_id=1, replica_groups=mesh['ctx'=8,'grp'=4] {'ctx'}, dimensions={0}, use_global_device_ids=true | all-gather | bytes 294912 | tf_op jit(solution)/shard_map/all_gather | solution.py:10
  85.4 4.0 copy.192
  91.6 54.4 %gather_fusion = f32[16384,64]{1,0:T(8,128)} fusion(f32[64,128]{0,1:T(8,128)S(1)} %copy.197, s32[16384]{0:T(1024)S(1)} %fusion.46), kind=kCustom, calls=%fused_computation | custom fusion | bytes 8454144 | tf_op jit(solution)/shard_map/jit(_take)/gather | solution.py:58
  146.7 9.9 %select_bitcast_fusion = f32[64,128,128]{0,2,1:T(8,128)} fusion(f32[128,128,64]{2,1,0:T(8,128)} %bitcast.218, pred[128,128]{1,0:T(8,128)(4,1)S(1)} %fusion.49), kind=kLoop, calls=%fused_computation.15 | loop fusion | flops 1048576 | bytes 8404992 | tf_op jit(solution)/shard_map/jit(_take)/select_n | solution.py:58
  156.6 7.4 %copy.198 = f32[64,128,128]{2,1,0:T(8,128)} copy(f32[64,128,128]{0,2,1:T(8,128)} %select_bitcast_fusion) | data formatting | bytes 8388608 | tf_op jit(solution)/shard_map/jit(_take)/select_n | solution.py:58
  164.0 10.1 %all_gather.22 = bf16[8,64,16]{1,2,0:T(8,128)(2,1)} all-gather(bf16[1,64,16]{1,2,0:T(8,128)(2,1)S(1)} %copy-done.39), channel_id=1, replica_groups=mesh['ctx'=8,'grp'=4] {'ctx'}, dimensions={0}, use_global_device_ids=true | all-gather | bytes 18432 | tf_op jit(solution)/shard_map/all_gather | solution.py:10
  180.7 10.1 %collective-permute-done.6 = bf16[512,1024]{1,0:T(8,128)(2,1)S(1)} collective-permute-done((bf16[512,1024]{1,0:T(8,128)(2,1)}, bf16[512,1024]{1,0:T(8,128)(2,1)S(1)}, u32[]{:S(2)}, u32[]{:S(2)}) %collective-permute-start.6) | collective-permute-done | bytes 1048608 | tf_op jit(solution)/shard_map/ppermute | solution.py:82
  191.9 2.3 constant_dynamic-update-slice_fusion.14
  194.1 2.4 constant_dynamic-update-slice_fusion.13
  196.5 2.4 constant_dynamic-update-slice_fusion.12
  198.8 2.3 constant_dynamic-update-slice_fusion.11
  201.1 2.3 constant_dynamic-update-slice_fusion.10
  206.6 2.2 constant_dynamic-update-slice_fusion.6
  208.8 2.2 constant_dynamic-update-slice_fusion.5
  211.1 2.3 constant_dynamic-update-slice_fusion.4
  213.4 2.3 constant_dynamic-update-slice_fusion.3
  215.7 2.3 constant_dynamic-update-slice_fusion.2
  220.1 13.3 %fusion.10 = f32[1024,1024]{1,0:T(8,128)S(1)} fusion(bf16[1024,4096]{1,0:T(8,128)(2,1)} %all-gather.2.cloned.1.call-done, bf16[8192,1024]{1,0:T(8,128)(2,1)} %constant_dynamic-update-slice_fusion, s32[]{:T(128)S(6)} %select_n.94), kind=kOutput, calls=%fused_computation.18 | convolution fusion | flops 8589934592 | bytes 20971524 | tf_op jit(solution)/shard_map/dot_general | solution.py:103
  236.4 7.0 %fusion.13 = f32[8,64,16,16]{3,2,1,0:T(8,128)S(1)} fusion(f32[8,128,64,16]{1,0,3,2:T(8,128)S(1)} %bitcast.214, f32[8,128]{1,0:T(8,128)S(1)} %get-tuple-element.384, f32[64,16,128]{2,1,0:T(8,128)S(1)} %get-tuple-element.370), kind=kOutput, calls=%fused_computation.21 | convolution fusion | flops 202375168 | bytes 5246976 | tf_op jit(solution)/shard_map/bgnt,btgc->bgcn/dot_general | solution.py:107
  245.4 2.4 fusion.43
  249.5 10.8 %all_gather.23 = bf16[8,64,16,16]{1,3,2,0:T(8,128)(2,1)} all-gather(bf16[1,64,16,16]{1,3,2,0:T(8,128)(2,1)} %copy.225), channel_id=1, replica_groups=mesh['ctx'=8,'grp'=4] {'ctx'}, dimensions={0}, use_global_device_ids=true | all-gather | bytes 294912 | tf_op jit(solution)/shard_map/all_gather | solution.py:10
  260.3 13.0 %while.31 = (s32[]{:T(128)}, f32[64,16,16]{0,2,1:T(8,128)S(1)}, s32[]{:T(128)}, bf16[8,64,16]{1,2,0:T(8,128)(2,1)}, bf16[8,64,16,16]{1,3,2,0:T(8,128)(2,1)}, /*index=5*/s32[]{:T(128)}, s32[]{:T(128)}, s32[]{:T(128)}, s32[]{:T(128)}) while((s32[]{:T(128)}, f32[64,16,16]{0,2,1:T(8,128)S(1)}, s32[]{:T(128)}, ...), condition=%wide.region_8.9_spmd.clone, body=%wide.region_7.8_spmd.clone.sunk | while | flops 82952 | bytes 174247 | solution.py:28
  274.3 3.8 bitcast_dynamic-update-slice_fusion.7
  284.4 5.2 fusion.15
  289.6 28.8 %fusion.2 = f32[8,64,16,128]{3,2,1,0:T(8,128)S(1)} fusion(f32[8,128,128]{2,1,0:T(8,128)S(1)} %copy-done.13, f32[64,128,128]{2,1,0:T(8,128)S(1)} %copy-done, f32[8,128,64,16]{1,0,3,2:T(8,128)S(1)} %bitcast.215), kind=kOutput, calls=%fused_computation.7 | convolution fusion | flops 1619001344 | bytes 13107200 | tf_op jit(solution)/shard_map/bgts,btgc->bsgc/dot_general | solution.py:106
  318.4 26.4 %add_bitcast_fusion.1 = f32[8,128,64,16]{1,3,2,0:T(8,128)S(1)} fusion(f32[8,64,16,128]{3,2,1,0:T(8,128)S(1)} %fusion.15, f32[8,128,128]{2,1,0:T(8,128)S(1)} %copy-done.14, f32[64,128,128]{2,1,0:T(8,128)S(1)} %copy-done, bf16[8,128,64,16]{1,0,3,2:T(8,128)(2,1)S(1)} %bitcast.217), kind=kOutput, calls=%fused_computation.43 | convolution fusion | flops 1620049920 | bytes 15204352 | tf_op jit(solution)/shard_map/bgts,bsgc->btgc/dot_general | solution.py:90
  344.8 2.4 copy.219
  347.4 5.0 add_bitcast_fusion
  352.5 2.4 copy.228
  355.3 7.1 %fusion.22 = (bf16[1024,1024]{0,1:T(8,128)(2,1)}, bf16[1024,1024]{0,1:T(8,128)(2,1)}, bf16[1024,1024]{0,1:T(8,128)(2,1)}, bf16[1024,1024]{0,1:T(8,128)(2,1)S(1)}) fusion(bf16[1024,1024]{0,1:T(8,128)(2,1)S(1)} %copy-done.6, bf16[1024,1024]{0,1:T(8,128)(2,1)S(1)} %copy-done.9, f32[1024,1024]{1,0:T(8,128)S(1)} %copy-done.11, f32[1024]{0:T(1024)S(1)} %copy-done.42, ...), kind=kLoop, calls=%fused_computation.35 | loop fusion | flops 19922944 | bytes 27267072 | tf_op jit(solution)/shard_map/convert_element_type | solution.py:130
  363.7 14.2 %convert_bitcast_fusion = bf16[4096,1024]{0,1:T(8,128)(2,1)} fusion(bf16[1024,1024]{0,1:T(8,128)(2,1)S(1)} %get-tuple-element.359, bf16[1024,4096]{1,0:T(8,128)(2,1)} %all-gather.2.cloned.1.call-done), kind=kOutput, calls=%fused_computation.16 | convolution fusion | flops 8594128896 | bytes 18874368 | tf_op jit(solution)/shard_map/dot_general | solution.py:131
  379.5 14.6 %convolution_convert_fusion = bf16[1024,4096]{1,0:T(8,128)(2,1)} fusion(bf16[1024,1024]{0,1:T(8,128)(2,1)S(1)} %copy-done.28, bf16[8192,1024]{1,0:T(8,128)(2,1)} %constant_dynamic-update-slice_fusion, s32[]{:T(128)S(6)} %select_n.94), kind=kOutput, calls=%fused_computation.17 | convolution fusion | flops 8594128896 | bytes 18874372 | tf_op jit(solution)/shard_map/dot_general | solution.py:121
  394.1 4.1 copy.229
  398.2 3.9 copy.230
  402.2 2.5 copy.231
  404.7 45.0 %reduce-scatter.5.cloned.1.call-done = bf16[512,1024]{0,1:T(8,128)(2,1)} async-done(((bf16[4096,1024]{0,1:T(8,128)(2,1)}), bf16[512,1024]{0,1:T(8,128)(2,1)}) %reduce-scatter.5.cloned.1.call-update) | async-done | bytes 1048592 | tf_op jit(solution)/shard_map/reduce_scatter | solution.py:134
  449.7 2.6 copy.232
  452.2 145.0 %reduce-scatter.3.cloned.1.call-done = bf16[1024,1024]{1,0:T(8,128)(2,1)} async-done(((bf16[1024,4096]{1,0:T(8,128)(2,1)}), bf16[1024,1024]{1,0:T(8,128)(2,1)}) %reduce-scatter.3.cloned.1.call-update) | async-done | bytes 2097168 | tf_op jit(solution)/shard_map/reduce_scatter | solution.py:125
  (203 shorter events, 58.5 us)
Async XLA Ops:
  7.2 212.9 %all-gather.2.cloned.1.call-start = ((), (), s32[]{:S(2)}) async-start(), calls=%async_computation.3 | async-start | bytes 10485760 | tf_op jit(solution)/shard_map/all_gather | solution.py:102
  7.9 441.8 %reduce-scatter.5.cloned.1.call-start = ((), (), s32[]{:S(2)}) async-start(), calls=%async_computation.4 | async-start | bytes 9437184 | tf_op jit(solution)/shard_map/reduce_scatter | solution.py:134
  7.9 16.1 %collective-permute-start = (bf16[512,1024]{1,0:T(8,128)(2,1)}, bf16[512,1024]{1,0:T(8,128)(2,1)S(1)}, u32[]{:S(2)}, u32[]{:S(2)}) collective-permute-start(bf16[512,1024]{1,0:T(8,128)(2,1)} %param.19), channel_id=1, source_target_pairs={{0,4},{4,8},{8,12},{12,16},{16,20},{20,24},{24,28},{28,0},{1,5},{5... | collective-permute-start | bytes 3145736 | tf_op jit(solution)/shard_map/ppermute | solution.py:82
  8.5 7.5 %copy-start.45 = (s32[4]{0:T(128)S(1)}, s32[4]{0:T(128)}, u32[]{:S(2)}) copy-start(s32[4]{0:T(128)} %param.20) | copy-start | bytes 52
  8.5 15.9 %copy-start.40 = (f32[64,16]{0,1:T(8,128)S(1)}, f32[64,16]{0,1:T(8,128)}, u32[]{:S(2)}) copy-start(f32[64,16]{0,1:T(8,128)} %param.16) | copy-start | bytes 12292
  8.5 15.9 %copy-start.41 = (f32[64,16]{0,1:T(8,128)S(1)}, f32[64,16]{0,1:T(8,128)}, u32[]{:S(2)}) copy-start(f32[64,16]{0,1:T(8,128)} %param.17) | copy-start | bytes 12292
  11.4 17.2 %copy-start.5 = (bf16[1024,1024]{0,1:T(8,128)(2,1)}, bf16[1024,1024]{0,1:T(8,128)(2,1)S(1)}, u32[]{:S(2)}) copy-start(bf16[1024,1024]{0,1:T(8,128)(2,1)S(1)} %copy.193) | copy-start | bytes 6291460
  24.0 18.9 %copy-start.25 = (bf16[512,1024]{1,0:T(8,128)(2,1)}, bf16[512,1024]{1,0:T(8,128)(2,1)S(1)}, u32[]{:S(2)}) copy-start(bf16[512,1024]{1,0:T(8,128)(2,1)S(1)} %collective-permute-done) | copy-start | bytes 3145732
  24.0 15.2 %collective-permute-start.1 = (bf16[512,1024]{1,0:T(8,128)(2,1)S(1)}, bf16[512,1024]{1,0:T(8,128)(2,1)}, u32[]{:S(2)}, u32[]{:S(2)}) collective-permute-start(bf16[512,1024]{1,0:T(8,128)(2,1)S(1)} %collective-permute-done), channel_id=1, source_target_pairs={{0,4},{4,8},{8,12},{12,16},{16,20},{20,24},{24,28},{28,0},{1,5},{5... | collective-permute-start | bytes 3145736 | tf_op jit(solution)/shard_map/ppermute | solution.py:82
  24.2 18.7 %copy-start.43 = (s32[8]{0:T(128)}, s32[8]{0:T(128)S(1)}, u32[]{:S(2)}) copy-start(s32[8]{0:T(128)S(1)} %slice_reduce_fusion) | copy-start | bytes 100
  24.3 18.6 %copy-start.44 = (s32[8]{0:T(128)}, s32[8]{0:T(128)S(1)}, u32[]{:S(2)}) copy-start(s32[8]{0:T(128)S(1)} %slice_reduce_fusion.1) | copy-start | bytes 100
  39.3 15.4 %collective-permute-start.2 = (bf16[512,1024]{1,0:T(8,128)(2,1)}, bf16[512,1024]{1,0:T(8,128)(2,1)}, u32[]{:S(2)}, u32[]{:S(2)}) collective-permute-start(bf16[512,1024]{1,0:T(8,128)(2,1)} %collective-permute-done.1), channel_id=1, source_target_pairs={{0,4},{4,8},{8,12},{12,16},{16,20},{20,24},{24,28},{28,0},{1,5},{5... | collective-permute-start | bytes 3145736 | tf_op jit(solution)/shard_map/ppermute | solution.py:82
  43.8 19.4 %copy-start.31 = (f32[64,16]{1,0:T(8,128)}, f32[64,16]{1,0:T(8,128)S(1)}, u32[]{:S(2)}) copy-start(f32[64,16]{1,0:T(8,128)S(1)} %copy.204) | copy-start | bytes 12292
  43.9 19.3 %copy-start.33 = (f32[64,16]{1,0:T(8,128)}, f32[64,16]{1,0:T(8,128)S(1)}, u32[]{:S(2)}) copy-start(f32[64,16]{1,0:T(8,128)S(1)} %copy.206) | copy-start | bytes 12292
  44.6 18.6 %copy-start.29 = (f32[64,16]{1,0:T(8,128)}, f32[64,16]{1,0:T(8,128)S(1)}, u32[]{:S(2)}) copy-start(f32[64,16]{1,0:T(8,128)S(1)} %copy.201) | copy-start | bytes 12292
  44.7 18.5 %copy-start.35 = (f32[64,16]{1,0:T(8,128)}, f32[64,16]{1,0:T(8,128)S(1)}, u32[]{:S(2)}) copy-start(f32[64,16]{1,0:T(8,128)S(1)} %copy.202) | copy-start | bytes 12292
  44.8 18.5 %copy-start.37 = (f32[64,16]{1,0:T(8,128)}, f32[64,16]{1,0:T(8,128)S(1)}, u32[]{:S(2)}) copy-start(f32[64,16]{1,0:T(8,128)S(1)} %copy.200) | copy-start | bytes 12292
  54.7 28.5 %collective-permute-start.3 = (bf16[512,1024]{1,0:T(8,128)(2,1)}, bf16[512,1024]{1,0:T(8,128)(2,1)}, u32[]{:S(2)}, u32[]{:S(2)}) collective-permute-start(bf16[512,1024]{1,0:T(8,128)(2,1)} %collective-permute-done.2), channel_id=1, source_target_pairs={{0,4},{4,8},{8,12},{12,16},{16,20},{20,24},{24,28},{28,0},{1,5},{5... | collective-permute-start | bytes 3145736 | tf_op jit(solution)/shard_map/ppermute | solution.py:82
  83.2 62.9 %collective-permute-start.4 = (bf16[512,1024]{1,0:T(8,128)(2,1)}, bf16[512,1024]{1,0:T(8,128)(2,1)}, u32[]{:S(2)}, u32[]{:S(2)}) collective-permute-start(bf16[512,1024]{1,0:T(8,128)(2,1)} %collective-permute-done.3), channel_id=1, source_target_pairs={{0,4},{4,8},{8,12},{12,16},{16,20},{20,24},{24,28},{28,0},{1,5},{5... | collective-permute-start | bytes 3145736 | tf_op jit(solution)/shard_map/ppermute | solution.py:82
  146.1 29.1 %collective-permute-start.5 = (bf16[512,1024]{1,0:T(8,128)(2,1)}, bf16[512,1024]{1,0:T(8,128)(2,1)}, u32[]{:S(2)}, u32[]{:S(2)}) collective-permute-start(bf16[512,1024]{1,0:T(8,128)(2,1)} %collective-permute-done.4), channel_id=1, source_target_pairs={{0,4},{4,8},{8,12},{12,16},{16,20},{20,24},{24,28},{28,0},{1,5},{5... | collective-permute-start | bytes 3145736 | tf_op jit(solution)/shard_map/ppermute | solution.py:82
  156.6 7.4 %copy-start.39 = (bf16[1,64,16]{1,2,0:T(8,128)(2,1)S(1)}, bf16[1,64,16]{1,2,0:T(8,128)(2,1)}, u32[]{:S(2)}) copy-start(bf16[1,64,16]{1,2,0:T(8,128)(2,1)} %get-tuple-element.364) | copy-start | bytes 6148
  156.6 20.3 %copy-start.34 = (f32[64,16]{1,0:T(8,128)S(1)}, f32[64,16]{1,0:T(8,128)}, u32[]{:S(2)}) copy-start(f32[64,16]{1,0:T(8,128)} %copy-done.33) | copy-start | bytes 12292
  164.0 15.3 %copy-start.32 = (f32[64,16]{1,0:T(8,128)S(1)}, f32[64,16]{1,0:T(8,128)}, u32[]{:S(2)}) copy-start(f32[64,16]{1,0:T(8,128)} %copy-done.31) | copy-start | bytes 12292
  175.2 15.6 %collective-permute-start.6 = (bf16[512,1024]{1,0:T(8,128)(2,1)}, bf16[512,1024]{1,0:T(8,128)(2,1)S(1)}, u32[]{:S(2)}, u32[]{:S(2)}) collective-permute-start(bf16[512,1024]{1,0:T(8,128)(2,1)} %collective-permute-done.5), channel_id=1, source_target_pairs={{0,4},{4,8},{8,12},{12,16},{16,20},{20,24},{24,28},{28,0},{1,5},{5... | collective-permute-start | bytes 3145736 | tf_op jit(solution)/shard_map/ppermute | solution.py:82
  180.7 32.7 %copy-start.17 = (f32[8,64,16,16]{3,2,1,0:T(8,128)}, f32[8,64,16,16]{3,2,1,0:T(8,128)S(1)}, u32[]{:S(2)}) copy-start(f32[8,64,16,16]{3,2,1,0:T(8,128)S(1)} %get-tuple-element.352) | copy-start | bytes 1572868
  194.1 9.3 %copy-start.26 = (bf16[512,1024]{1,0:T(8,128)(2,1)S(1)}, bf16[512,1024]{1,0:T(8,128)(2,1)}, u32[]{:S(2)}) copy-start(bf16[512,1024]{1,0:T(8,128)(2,1)} %copy-done.25) | copy-start | bytes 3145732
  196.5 8.0 %copy-start.24 = (bf16[512,1024]{1,0:T(8,128)(2,1)S(1)}, bf16[512,1024]{1,0:T(8,128)(2,1)}, u32[]{:S(2)}) copy-start(bf16[512,1024]{1,0:T(8,128)(2,1)} %param.19) | copy-start | bytes 3145732
  220.1 13.3 %copy-start.8 = (bf16[1024,1024]{0,1:T(8,128)(2,1)S(1)}, bf16[1024,1024]{0,1:T(8,128)(2,1)}, u32[]{:S(2)}) copy-start(bf16[1024,1024]{0,1:T(8,128)(2,1)} %copy.192) | copy-start | bytes 6291460
  236.3 7.1 %copy-start.3 = (f32[128,8,8,128]{3,2,1,0:T(8,128)}, f32[128,8,8,128]{3,2,1,0:T(8,128)S(1)}, u32[]{:S(2)}) copy-start(f32[128,8,8,128]{3,2,1,0:T(8,128)S(1)} %copy.235) | copy-start | bytes 12582916
  236.3 9.0 %copy-start.30 = (f32[64,16]{1,0:T(8,128)S(1)}, f32[64,16]{1,0:T(8,128)}, u32[]{:S(2)}) copy-start(f32[64,16]{1,0:T(8,128)} %copy-done.29) | copy-start | bytes 12292
  236.4 9.0 %copy-start.36 = (f32[64,16]{1,0:T(8,128)S(1)}, f32[64,16]{1,0:T(8,128)}, u32[]{:S(2)}) copy-start(f32[64,16]{1,0:T(8,128)} %copy-done.35) | copy-start | bytes 12292
  236.4 9.0 %copy-start.38 = (f32[64,16]{1,0:T(8,128)S(1)}, f32[64,16]{1,0:T(8,128)}, u32[]{:S(2)}) copy-start(f32[64,16]{1,0:T(8,128)} %copy.224) | copy-start | bytes 12292
  278.1 4.2 copy-start.21
  278.1 2.8 copy-start.18
  284.4 5.2 copy-start
  284.4 5.2 copy-start.4
  284.4 5.2 copy-start.13
  289.6 28.8 %copy-start.14 = (f32[8,128,128]{2,1,0:T(8,128)S(1)}, f32[8,128,128]{2,1,0:T(8,128)}, u32[]{:S(2)}) copy-start(f32[8,128,128]{2,1,0:T(8,128)} %and_convert_fusion) | copy-start | bytes 1572868
  344.8 2.5 copy-start.16
  344.8 2.5 copy-start.23
  344.8 2.6 copy-start.20
  347.4 7.5 %copy-start.11 = (f32[1024,1024]{1,0:T(8,128)S(1)}, f32[1024,1024]{1,0:T(8,128)}, u32[]{:S(2)}) copy-start(f32[1024,1024]{1,0:T(8,128)} %copy-done.10) | copy-start | bytes 12582916
  352.4 2.5 copy-start.6
  352.4 2.5 copy-start.7
  352.4 2.8 copy-start.9
  352.5 2.8 copy-start.42
  377.9 219.3 %reduce-scatter.3.cloned.1.call-start = ((), (), s32[]{:S(2)}) async-start(), calls=%async_computation.2 | async-start | bytes 10485760 | tf_op jit(solution)/shard_map/reduce_scatter | solution.py:125
  394.1 8.1 %copy-start.12 = (bf16[1024,1024]{0,1:T(8,128)(2,1)S(1)}, bf16[1024,1024]{0,1:T(8,128)(2,1)}, u32[]{:S(2)}) copy-start(bf16[1024,1024]{0,1:T(8,128)(2,1)} %get-tuple-element.356) | copy-start | bytes 6291460
  (8 other events, 14.3 us)
Sparse Core Ops, SparseCore 0:
  9.6 152.3 all-gather.1
  378.1 71.5 reduce-scatter.4
  452.7 144.4 reduce-scatter.2
